TPU v7x, 512 devices: a whole 4x4x16 slice. The times are simulated.
512 devices in a mesh: req: 16 (over x, y_lo, core), blk: 32 (over z, y_hi).
Axes of the slice: x: 4, y: 4 (y_hi: 2, y_lo: 2; y = y_hi * 2 + y_lo), z: 16, core: 2. Of those that a mesh axis runs over, the one named last changes fastest.
Arguments:
- queries: bfloat16 [16, 32, 512, 512], P('req', 'blk'), may hold values from -6 to 6
- keys: bfloat16 [16, 32, 512, 256], P('req', 'blk'), may hold values from -25 to 25
- values: bfloat16 [16, 32, 512, 256], P('req', 'blk'), may hold values from -6 to 6
- block_map: int32 [16, 8, 2], P('req'), may hold values from 0 to 15, as said below
- lengths: int32 [16], P('req'), may hold values from 1024 to 4096
- group_of_prompt: int32 [16], replicated, may hold values from 0 to 15, each once
- decode_rank: int32 [16, 32], P('req'), may hold values from 0 to 31, as said below
Outputs:
- attended: bfloat16 [16, 32, 512, 512], P('req', 'blk')
- cache: bfloat16 [16, 4096, 2048], P('req', 'blk')
Inputs may be any that keep to these rules, and one draw needn't show every extreme that they name: In each group, block_map[g] holds each of 0 to 15 once, and the two halves of each slot hold blocks b and 15 - b, in either order. `decode_rank`: each group's row holds each of 0 to 31 once.
All inputs are finite; a program needn't handle non-finite values.
Results may differ from a plain program's by a relative error of at most 0.0098.
Values may be sent and summed in bfloat16 or wider, within the bound.
A program may use at most 64 MiB of HBM per device.

v0:
```python
import math

import jax
import jax.numpy as jnp
from jax import lax
from jax.sharding import PartitionSpec as P

QUERY_HEADS = 16
KEY_VALUE_HEADS = 8
HEAD_SIZE = 128
HEAD_DIVISIONS = 4
Q_DEV = 4
KV_DEV = 2


cap_value = 50.0
query_scale = 1.0 / 12.0
rope_base = 10000.0


def shifted(shard, axis, by):
    peers = lax.axis_size(axis)
    return lax.ppermute(shard, axis, [(i, (i + by) % peers) for i in range(peers)])


def apply_rotary(row_block, token_position, head_count):
    row_count = row_block.shape[0]
    head_width = row_block.shape[1] // head_count
    half_width = head_width // 2
    shaped = row_block.astype(jnp.float32).reshape(row_count, head_count, head_width)
    frequency = jnp.exp(
        -math.log(rope_base) * (2.0 * jnp.arange(half_width, dtype=jnp.float32)) / head_width
    )
    angles = token_position.astype(jnp.float32)[:, None] * frequency[None, :]
    cosine = jnp.cos(angles)[:, None, :]
    sine_part = jnp.sin(angles)[:, None, :]
    front_half = shaped[:, :, :half_width]
    second = shaped[:, :, half_width:]
    turned = jnp.concatenate(
        [front_half * cosine - second * sine_part, second * cosine + front_half * sine_part], axis=2
    )
    return turned.reshape(row_count, head_count * head_width)


def slot_positions(table, slot, block_len):
    slot_ids = jnp.arange(table.shape[0], dtype=jnp.int32)
    chosen = jnp.sum(jnp.where((slot_ids == slot)[:, None], table, 0), axis=0)
    return chosen[:, None] * block_len + jnp.arange(block_len, dtype=jnp.int32)[None, :]


def forward_step(buffer):
    return shifted(buffer, "blk", HEAD_DIVISIONS)


def on_device(queries, keys, values, block_map, lengths, group_of_prompt, decode_rank):
    token_rows = queries.shape[2]
    block_len = token_rows // 2
    rank_count = lax.axis_size("blk")
    cache_slot_count = rank_count // HEAD_DIVISIONS
    member = lax.axis_index("blk")
    own_slot = member // HEAD_DIVISIONS
    group_id = lax.axis_index("req")
    group_portion = QUERY_HEADS // KEY_VALUE_HEADS
    kv_dev_width = KV_DEV * HEAD_SIZE
    all_lengths = lax.all_gather(lengths, "req", axis=0, tiled=True)
    length = jnp.sum(jnp.where(group_of_prompt == group_id, all_lengths, 0))
    table = block_map[0]
    own_pos = slot_positions(table, own_slot, block_len)
    flat_pos = own_pos.reshape(-1)
    query_rot = (apply_rotary(queries[0, 0], flat_pos, Q_DEV) * query_scale).astype(jnp.bfloat16)
    rotated_key = apply_rotary(keys[0, 0], flat_pos, KV_DEV).astype(jnp.bfloat16)
    value_row_list = values[0, 0]
    query_halves = query_rot.reshape(2, block_len, KV_DEV, group_portion, HEAD_SIZE)

    def attend_tile(numerator, denominator, portion, key_sub, value_sub, key_pos):
        scores = jnp.einsum(
            "qkgd,nkd->kgqn", query_halves[portion], key_sub, preferred_element_type=jnp.float32
        )
        capped = cap_value * jnp.tanh(scores / cap_value)
        allowed = key_pos[None, :] <= own_pos[portion][:, None]
        expo_vals = jnp.where(allowed[None, None], jnp.exp(capped), 0.0)
        weight = expo_vals.astype(jnp.bfloat16)
        numerator = numerator + jnp.einsum(
            "kgqn,nkd->qkgd", weight, value_sub, preferred_element_type=jnp.float32
        )
        denominator = denominator + jnp.sum(expo_vals, axis=3)
        return (numerator, denominator)

    def absorb(totals, packet, slot):
        numerator, denominator = totals
        key_pos = slot_positions(table, slot, block_len)
        key_blocks = packet[0].reshape(2, block_len, KV_DEV, HEAD_SIZE)
        value_blocks = packet[1].reshape(2, block_len, KV_DEV, HEAD_SIZE)
        new_numer = []
        new_denom = []
        for portion in range(2):
            result_pair = (numerator[portion], denominator[portion])
            for half in range(2):
                result_pair = attend_tile(
                    result_pair[0],
                    result_pair[1],
                    portion,
                    key_blocks[half],
                    value_blocks[half],
                    key_pos[half],
                )
            new_numer.append(result_pair[0])
            new_denom.append(result_pair[1])
        return (jnp.stack(new_numer), jnp.stack(new_denom))

    packet = jnp.stack([rotated_key, value_row_list])
    start_numer = jnp.zeros((2, block_len, KV_DEV, group_portion, HEAD_SIZE), jnp.float32)
    start_denom = jnp.zeros((2, KV_DEV, group_portion, block_len), jnp.float32)
    numerator, denominator = absorb((start_numer, start_denom), packet, own_slot)

    def step_single(turn, carry):
        numer_now, denom_now, buffer = carry
        buffer = forward_step(buffer)
        numer_now, denom_now = absorb(
            (numer_now, denom_now), buffer, (own_slot - turn) % cache_slot_count
        )
        return (numer_now, denom_now, buffer)

    numerator, denominator, _ = lax.fori_loop(
        1, cache_slot_count, step_single, (numerator, denominator, packet)
    )
    safe_denom = jnp.where(denominator > 0.0, denominator, 1.0)
    output = numerator / jnp.transpose(safe_denom, (0, 3, 1, 2))[..., None]
    output = output.reshape(token_rows, Q_DEV * HEAD_SIZE)
    live = flat_pos < length
    attended = jnp.where(live[:, None], output, 0.0).astype(jnp.bfloat16)
    joined = jnp.concatenate([rotated_key, value_row_list], axis=1)
    kept_rows = jnp.where(live[:, None], joined, jnp.zeros_like(joined))
    rank_portion = block_len // rank_count
    shaped = kept_rows.reshape(2, rank_portion, rank_count, 2 * kv_dev_width)
    rank_of = decode_rank[0]
    rank_ids = jnp.arange(rank_count, dtype=jnp.int32)
    inverse = jnp.sum(
        jnp.where(rank_of[None, :] == rank_ids[:, None], rank_ids[None, :], 0), axis=1
    )
    outgoing = jnp.take(shaped, inverse, axis=2)
    arrived = lax.all_to_all(outgoing, "blk", split_axis=2, concat_axis=2, tiled=True)
    regrouped = arrived.reshape(2, rank_portion, cache_slot_count, HEAD_DIVISIONS, 2, kv_dev_width)
    regrouped = jnp.transpose(regrouped, (2, 0, 1, 4, 3, 5)).reshape(
        cache_slot_count * 2 * rank_portion, 2 * KEY_VALUE_HEADS * HEAD_SIZE
    )
    target = (
        table.reshape(-1)[:, None] * rank_portion
        + jnp.arange(rank_portion, dtype=jnp.int32)[None, :]
    )
    cache_rows = (
        jnp.zeros((token_rows // HEAD_DIVISIONS, 2 * KEY_VALUE_HEADS * HEAD_SIZE), jnp.bfloat16)
        .at[target.reshape(-1)]
        .set(regrouped)
    )
    return (attended[None, None], cache_rows[None])


def solution(mesh):
    placed = (
        P("req", "blk", None, None),
        P("req", "blk", None, None),
        P("req", "blk", None, None),
        P("req", None, None),
        P("req"),
        P(),
        P("req", None),
    )
    return jax.shard_map(
        on_device,
        mesh=mesh,
        in_specs=placed,
        out_specs=(P("req", "blk", None, None), P("req", "blk", None)),
        check_vma=False,
    )
```

profile of v0, /device:TPU:16, one launch (start us, length us, event | category | flops | bytes accessed | tf_op | source)
XLA Modules:
  0.0 276.7 jit_solution(10896126467494985319)
XLA Ops:
  2.3 1.1 copy.148
  5.4 1.3 dynamic-slice
  6.7 0.8 dynamic-update-slice
  7.4 12.1 %all-reduce = s32[16]{0:T(128)S(1)} all-reduce(s32[16]{0:T(128)S(1)} %dynamic-update-slice), channel_id=1, replica_groups=mesh['req'=16,'blk'=32] {'req'}, use_global_device_ids=true, to_apply=%add | all-reduce | flops 16 | bytes 128
  23.2 0.9 select_bitcast_fusion
  24.1 18.2 %all-to-all-start = ((bf16[2,8,32,512]{3,1,0,2:T(8,128)(2,1)}), bf16[2,8,32,512]{3,1,0,2:T(8,128)(2,1)S(1)}, u32[]{:S(2)}, u32[]{:S(2)}) async-start(bf16[2,8,32,512]{3,1,0,2:T(8,128)(2,1)} %select_bitcast_fusion), calls=%async_computation | async-start | bytes 1048576 | tf_op jit(solution)/shard_map/all_to_all | solution.py:142
  42.6 0.7 copy-done.1
  48.2 222.1 %while.19 = (s32[]{:T(128)}, f32[2,256,2,2,128]{4,1,3,2,0:T(8,128)S(1)}, f32[2,2,2,256]{3,2,1,0:T(2,128)S(1)}, bf16[2,512,256]{1,2,0:T(8,128)(2,1)S(1)}, s32[]{:...) while((s32[]{:T(128)}, ...), condition=%wide.region_12.13_spmd, body=%wide.region_6.0_spmd.sunk | while | flops 543164992 | bytes 17381768 | solution.py:124
  48.2 4.3 %collective-permute-start = (bf16[2,512,256]{1,2,0:T(8,128)(2,1)S(1)}, bf16[2,512,256]{1,2,0:T(8,128)(2,1)S(1)}, u32[]{:S(2)}, u32[]{:S(2)}) collective-permute-start(bf16[2,512,256]{1,2,0:T(8,128)(2,1)S(1)} %get-tuple-element.428), channel_id=1, source_target_pairs={{0,4},{1,5},{2,6},{3,7},{4,8},{5,9},{6,10},{7,11},{8,12},{9,13},{1... | collective-permute-start | bytes 1572872 | tf_op jit(solution)/shard_map/while/body/eval_jaxpr/ppermute | solution.py:23
  52.9 31.1 %collective-permute-done = bf16[2,512,256]{1,2,0:T(8,128)(2,1)S(1)} collective-permute-done((bf16[2,512,256]{1,2,0:T(8,128)(2,1)S(1)}, bf16[2,512,256]{1,2,0:T(8,128)(2,1)S(1)}, u32[]{:S(2)}, u32[]{:S(2)}) %collective-permute-start) | collective-permute-done | bytes 524320 | tf_op jit(solution)/shard_map/while/body/eval_jaxpr/ppermute | solution.py:23
  87.9 1.9 collective-permute-start
  90.3 17.8 %collective-permute-done = bf16[2,512,256]{1,2,0:T(8,128)(2,1)S(1)} collective-permute-done((bf16[2,512,256]{1,2,0:T(8,128)(2,1)S(1)}, bf16[2,512,256]{1,2,0:T(8,128)(2,1)S(1)}, u32[]{:S(2)}, u32[]{:S(2)}) %collective-permute-start) | collective-permute-done | bytes 524320 | tf_op jit(solution)/shard_map/while/body/eval_jaxpr/ppermute | solution.py:23
  111.9 8.9 %collective-permute-start = (bf16[2,512,256]{1,2,0:T(8,128)(2,1)S(1)}, bf16[2,512,256]{1,2,0:T(8,128)(2,1)S(1)}, u32[]{:S(2)}, u32[]{:S(2)}) collective-permute-start(bf16[2,512,256]{1,2,0:T(8,128)(2,1)S(1)} %get-tuple-element.428), channel_id=1, source_target_pairs={{0,4},{1,5},{2,6},{3,7},{4,8},{5,9},{6,10},{7,11},{8,12},{9,13},{1... | collective-permute-start | bytes 1572872 | tf_op jit(solution)/shard_map/while/body/eval_jaxpr/ppermute | solution.py:23
  121.3 19.4 %collective-permute-done = bf16[2,512,256]{1,2,0:T(8,128)(2,1)S(1)} collective-permute-done((bf16[2,512,256]{1,2,0:T(8,128)(2,1)S(1)}, bf16[2,512,256]{1,2,0:T(8,128)(2,1)S(1)}, u32[]{:S(2)}, u32[]{:S(2)}) %collective-permute-start) | collective-permute-done | bytes 524320 | tf_op jit(solution)/shard_map/while/body/eval_jaxpr/ppermute | solution.py:23
  144.5 8.8 %collective-permute-start = (bf16[2,512,256]{1,2,0:T(8,128)(2,1)S(1)}, bf16[2,512,256]{1,2,0:T(8,128)(2,1)S(1)}, u32[]{:S(2)}, u32[]{:S(2)}) collective-permute-start(bf16[2,512,256]{1,2,0:T(8,128)(2,1)S(1)} %get-tuple-element.428), channel_id=1, source_target_pairs={{0,4},{1,5},{2,6},{3,7},{4,8},{5,9},{6,10},{7,11},{8,12},{9,13},{1... | collective-permute-start | bytes 1572872 | tf_op jit(solution)/shard_map/while/body/eval_jaxpr/ppermute | solution.py:23
  153.8 17.7 %collective-permute-done = bf16[2,512,256]{1,2,0:T(8,128)(2,1)S(1)} collective-permute-done((bf16[2,512,256]{1,2,0:T(8,128)(2,1)S(1)}, bf16[2,512,256]{1,2,0:T(8,128)(2,1)S(1)}, u32[]{:S(2)}, u32[]{:S(2)}) %collective-permute-start) | collective-permute-done | bytes 524320 | tf_op jit(solution)/shard_map/while/body/eval_jaxpr/ppermute | solution.py:23
  175.3 9.2 %collective-permute-start = (bf16[2,512,256]{1,2,0:T(8,128)(2,1)S(1)}, bf16[2,512,256]{1,2,0:T(8,128)(2,1)S(1)}, u32[]{:S(2)}, u32[]{:S(2)}) collective-permute-start(bf16[2,512,256]{1,2,0:T(8,128)(2,1)S(1)} %get-tuple-element.428), channel_id=1, source_target_pairs={{0,4},{1,5},{2,6},{3,7},{4,8},{5,9},{6,10},{7,11},{8,12},{9,13},{1... | collective-permute-start | bytes 1572872 | tf_op jit(solution)/shard_map/while/body/eval_jaxpr/ppermute | solution.py:23
  185.0 21.1 %collective-permute-done = bf16[2,512,256]{1,2,0:T(8,128)(2,1)S(1)} collective-permute-done((bf16[2,512,256]{1,2,0:T(8,128)(2,1)S(1)}, bf16[2,512,256]{1,2,0:T(8,128)(2,1)S(1)}, u32[]{:S(2)}, u32[]{:S(2)}) %collective-permute-start) | collective-permute-done | bytes 524320 | tf_op jit(solution)/shard_map/while/body/eval_jaxpr/ppermute | solution.py:23
  209.9 6.5 %collective-permute-start = (bf16[2,512,256]{1,2,0:T(8,128)(2,1)S(1)}, bf16[2,512,256]{1,2,0:T(8,128)(2,1)S(1)}, u32[]{:S(2)}, u32[]{:S(2)}) collective-permute-start(bf16[2,512,256]{1,2,0:T(8,128)(2,1)S(1)} %get-tuple-element.428), channel_id=1, source_target_pairs={{0,4},{1,5},{2,6},{3,7},{4,8},{5,9},{6,10},{7,11},{8,12},{9,13},{1... | collective-permute-start | bytes 1572872 | tf_op jit(solution)/shard_map/while/body/eval_jaxpr/ppermute | solution.py:23
  216.9 32.6 %collective-permute-done = bf16[2,512,256]{1,2,0:T(8,128)(2,1)S(1)} collective-permute-done((bf16[2,512,256]{1,2,0:T(8,128)(2,1)S(1)}, bf16[2,512,256]{1,2,0:T(8,128)(2,1)S(1)}, u32[]{:S(2)}, u32[]{:S(2)}) %collective-permute-start) | collective-permute-done | bytes 524320 | tf_op jit(solution)/shard_map/while/body/eval_jaxpr/ppermute | solution.py:23
  253.3 5.3 %collective-permute-start = (bf16[2,512,256]{1,2,0:T(8,128)(2,1)S(1)}, bf16[2,512,256]{1,2,0:T(8,128)(2,1)S(1)}, u32[]{:S(2)}, u32[]{:S(2)}) collective-permute-start(bf16[2,512,256]{1,2,0:T(8,128)(2,1)S(1)} %get-tuple-element.428), channel_id=1, source_target_pairs={{0,4},{1,5},{2,6},{3,7},{4,8},{5,9},{6,10},{7,11},{8,12},{9,13},{1... | collective-permute-start | bytes 1572872 | tf_op jit(solution)/shard_map/while/body/eval_jaxpr/ppermute | solution.py:23
  259.1 7.4 %collective-permute-done = bf16[2,512,256]{1,2,0:T(8,128)(2,1)S(1)} collective-permute-done((bf16[2,512,256]{1,2,0:T(8,128)(2,1)S(1)}, bf16[2,512,256]{1,2,0:T(8,128)(2,1)S(1)}, u32[]{:S(2)}, u32[]{:S(2)}) %collective-permute-start) | collective-permute-done | bytes 524320 | tf_op jit(solution)/shard_map/while/body/eval_jaxpr/ppermute | solution.py:23
  272.4 1.0 select_convert_fusion
  274.6 2.1 scatter_custom_fusion
  (216 shorter events, 43.6 us)
Async XLA Ops:
  0.7 0.7 copy-start.4
  1.5 0.7 copy-start.2
  4.6 15.0 %copy-start = (bf16[1,1,512,256]{3,2,1,0:T(8,128)(2,1)S(1)}, bf16[1,1,512,256]{3,2,1,0:T(8,128)(2,1)}, u32[]{:S(2)}) copy-start(bf16[1,1,512,256]{3,2,1,0:T(8,128)(2,1)} %param.11) | copy-start | bytes 786436
  20.5 0.7 copy-start.3
  24.1 249.3 %all-to-all-start = ((bf16[2,8,32,512]{3,1,0,2:T(8,128)(2,1)}), bf16[2,8,32,512]{3,1,0,2:T(8,128)(2,1)S(1)}, u32[]{:S(2)}, u32[]{:S(2)}) async-start(bf16[2,8,32,512]{3,1,0,2:T(8,128)(2,1)} %select_bitcast_fusion), calls=%async_computation | async-start | bytes 1048576 | tf_op jit(solution)/shard_map/all_to_all | solution.py:142
  42.3 1.0 copy-start.1
  48.2 35.9 %collective-permute-start = (bf16[2,512,256]{1,2,0:T(8,128)(2,1)S(1)}, bf16[2,512,256]{1,2,0:T(8,128)(2,1)S(1)}, u32[]{:S(2)}, u32[]{:S(2)}) collective-permute-start(bf16[2,512,256]{1,2,0:T(8,128)(2,1)S(1)} %get-tuple-element.428), channel_id=1, source_target_pairs={{0,4},{1,5},{2,6},{3,7},{4,8},{5,9},{6,10},{7,11},{8,12},{9,13},{1... | collective-permute-start | bytes 1572872 | tf_op jit(solution)/shard_map/while/body/eval_jaxpr/ppermute | solution.py:23
  87.9 20.2 %collective-permute-start = (bf16[2,512,256]{1,2,0:T(8,128)(2,1)S(1)}, bf16[2,512,256]{1,2,0:T(8,128)(2,1)S(1)}, u32[]{:S(2)}, u32[]{:S(2)}) collective-permute-start(bf16[2,512,256]{1,2,0:T(8,128)(2,1)S(1)} %get-tuple-element.428), channel_id=1, source_target_pairs={{0,4},{1,5},{2,6},{3,7},{4,8},{5,9},{6,10},{7,11},{8,12},{9,13},{1... | collective-permute-start | bytes 1572872 | tf_op jit(solution)/shard_map/while/body/eval_jaxpr/ppermute | solution.py:23
  111.9 28.8 %collective-permute-start = (bf16[2,512,256]{1,2,0:T(8,128)(2,1)S(1)}, bf16[2,512,256]{1,2,0:T(8,128)(2,1)S(1)}, u32[]{:S(2)}, u32[]{:S(2)}) collective-permute-start(bf16[2,512,256]{1,2,0:T(8,128)(2,1)S(1)} %get-tuple-element.428), channel_id=1, source_target_pairs={{0,4},{1,5},{2,6},{3,7},{4,8},{5,9},{6,10},{7,11},{8,12},{9,13},{1... | collective-permute-start | bytes 1572872 | tf_op jit(solution)/shard_map/while/body/eval_jaxpr/ppermute | solution.py:23
  144.5 27.0 %collective-permute-start = (bf16[2,512,256]{1,2,0:T(8,128)(2,1)S(1)}, bf16[2,512,256]{1,2,0:T(8,128)(2,1)S(1)}, u32[]{:S(2)}, u32[]{:S(2)}) collective-permute-start(bf16[2,512,256]{1,2,0:T(8,128)(2,1)S(1)} %get-tuple-element.428), channel_id=1, source_target_pairs={{0,4},{1,5},{2,6},{3,7},{4,8},{5,9},{6,10},{7,11},{8,12},{9,13},{1... | collective-permute-start | bytes 1572872 | tf_op jit(solution)/shard_map/while/body/eval_jaxpr/ppermute | solution.py:23
  175.3 30.8 %collective-permute-start = (bf16[2,512,256]{1,2,0:T(8,128)(2,1)S(1)}, bf16[2,512,256]{1,2,0:T(8,128)(2,1)S(1)}, u32[]{:S(2)}, u32[]{:S(2)}) collective-permute-start(bf16[2,512,256]{1,2,0:T(8,128)(2,1)S(1)} %get-tuple-element.428), channel_id=1, source_target_pairs={{0,4},{1,5},{2,6},{3,7},{4,8},{5,9},{6,10},{7,11},{8,12},{9,13},{1... | collective-permute-start | bytes 1572872 | tf_op jit(solution)/shard_map/while/body/eval_jaxpr/ppermute | solution.py:23
  209.9 39.7 %collective-permute-start = (bf16[2,512,256]{1,2,0:T(8,128)(2,1)S(1)}, bf16[2,512,256]{1,2,0:T(8,128)(2,1)S(1)}, u32[]{:S(2)}, u32[]{:S(2)}) collective-permute-start(bf16[2,512,256]{1,2,0:T(8,128)(2,1)S(1)} %get-tuple-element.428), channel_id=1, source_target_pairs={{0,4},{1,5},{2,6},{3,7},{4,8},{5,9},{6,10},{7,11},{8,12},{9,13},{1... | collective-permute-start | bytes 1572872 | tf_op jit(solution)/shard_map/while/body/eval_jaxpr/ppermute | solution.py:23
  253.3 13.2 %collective-permute-start = (bf16[2,512,256]{1,2,0:T(8,128)(2,1)S(1)}, bf16[2,512,256]{1,2,0:T(8,128)(2,1)S(1)}, u32[]{:S(2)}, u32[]{:S(2)}) collective-permute-start(bf16[2,512,256]{1,2,0:T(8,128)(2,1)S(1)} %get-tuple-element.428), channel_id=1, source_target_pairs={{0,4},{1,5},{2,6},{3,7},{4,8},{5,9},{6,10},{7,11},{8,12},{9,13},{1... | collective-permute-start | bytes 1572872 | tf_op jit(solution)/shard_map/while/body/eval_jaxpr/ppermute | solution.py:23
where the time goes:
time: 277 us
  waiting for transfers between devices  147 us (53%)
  starting transfers between devices  63.2 us (23%)
  matrix products  28.1 us (10%)
  local copies, waits for them, and re-layouts  13.5 us (5%)
  blocking collectives  12.1 us (4%)
  other arithmetic  9.92 us (4%)
    ppermute x7, waiting for transfers between devices, shifted(): lax.ppermute(shard, axis, [(i, (i + by) % peers) for i in range(peers)])  147 us
    ppermute x7, starting transfers between devices, shifted(): lax.ppermute(shard, axis, [(i, (i + by) % peers) for i in range(peers)])  45 us
    all_to_all x1, starting transfers between devices, on_device(): lax.all_to_all(outgoing, 'blk', split_axis=2, concat_axis=2, tiled=True)  18.2 us
    dot_general x32, matrix products, attend_tile(): jnp.einsum('qkgd,nkd->kgqn', query_halves[portion], key_sub, preferred_el...  17 us
    unnamed x1, blocking collectives  12.1 us
    dot_general x32, matrix products, attend_tile(): jnp.einsum('kgqn,nkd->qkgd', weight, value_sub, preferred_element_type=jn...  11.1 us
    unnamed x19, local copies, waits for them, and re-layouts  6.42 us
  transfers between devices with their start and end apart: 8, of which 7 were waited for; matrix products, arithmetic and copies ran while one was open for 13% of the time, Pallas kernels for 0%

commit v1 on v0

v1 whole, which is shorter than its diff:
```python
import functools
import math

import jax
import jax.numpy as jnp
from jax import lax
from jax.experimental import pallas as pl
from jax.experimental.pallas import tpu as pltpu
from jax.sharding import PartitionSpec as P

SLOTS = 8
HEAD_DIVISIONS = 4
KV_DEV = 2
HEAD = 128
HALF_TURN = 64
BLOCK = 256
RESIDUES = 32
CAP = 50.0
QUERY_SCALE = 1.0 / 12.0
ROPE_BASE = 10000.0
ORDER = (0, 1, 7, 2, 6, 3, 5, 4)
MESH = pl.DeviceIdType.MESH


def pick(condition, value):
    return jnp.where(condition, value, 0)


def kernel(
    q_hbm, k_hbm, v_hbm, table, length_ref, group_of, rank_of,
    out_ref, cache_ref,
    q_raw, kbuf, vbuf, qrot, krot, num, den, cos_row, sin_row, cos_blk, sin_blk,
    choose, chosen, arrived, lens,
    load_sem, send_sem, recv_sem, pick_send, pick_recv, len_send, len_recv,
):
    req = lax.axis_index("req")
    me = lax.axis_index("blk")
    slot = me // HEAD_DIVISIONS
    head_group = me % HEAD_DIVISIONS
    ring = SLOTS * HEAD_DIVISIONS
    right = (me + HEAD_DIVISIONS) % ring
    left = (me + ring - HEAD_DIVISIONS) % ring

    def quad_peer(e):
        low = head_group % 2
        high = head_group // 2
        if e & 1:
            low = 1 - low
        if e & 2:
            high = 1 - high
        return high * 2 + low

    core = req % 2
    y_low = (req // 2) % 2
    x = req // 4
    mate = req + 1 - 2 * core
    y_mate = req + 2 - 4 * y_low
    x_mates = [((x + i) % 4) * 4 + req % 4 for i in (1, 2, 3)]

    loads = [
        pltpu.make_async_copy(q_hbm, q_raw, load_sem.at[0]),
        pltpu.make_async_copy(k_hbm, kbuf.at[0], load_sem.at[1]),
        pltpu.make_async_copy(v_hbm, vbuf.at[0], load_sem.at[2]),
    ]
    for load in loads:
        load.start()

    barrier = pltpu.get_barrier_semaphore()
    partners = [(req, right), (req, left)]
    partners += [(req, slot * HEAD_DIVISIONS + quad_peer(e)) for e in (1, 2, 3)]
    partners += [(mate, me), (y_mate, me)] + [(xm, me) for xm in x_mates]
    for partner in partners:
        pl.semaphore_signal(barrier, inc=1, device_id=partner, device_id_type=MESH)
    pl.semaphore_wait(barrier, len(partners))

    def hop(side, turn, chunk):
        half = chunk // 2
        rows = pl.ds(half * BLOCK, BLOCK)
        is_value = chunk % 2 == 1
        buf = vbuf if is_value else kbuf
        if side == 0:
            source, target, device = turn, turn + 1, right
        else:
            source, target, device = (SLOTS - turn) % SLOTS, SLOTS - turn - 1, left
        if turn == 0:
            src = (v_hbm if is_value else k_hbm).at[rows]
        else:
            src = buf.at[source, rows]
        return pltpu.make_async_remote_copy(
            src_ref=src,
            dst_ref=buf.at[target, rows],
            send_sem=send_sem.at[side, turn, chunk],
            recv_sem=recv_sem.at[target, chunk],
            device_id=(req, device),
            device_id_type=MESH,
        )

    def travels(side, turn, chunk):
        if turn < 3:
            return True
        return turn == 3 and (chunk // 2 == side)

    sent = []
    for chunk in range(4):
        for side in range(2):
            copy = hop(side, 0, chunk)
            copy.start()
            sent.append(copy)

    lens[req] = jnp.full((8, 128), length_ref[0], jnp.int32)

    def len_copy(index, start, size, to):
        rows = lens.at[pl.ds(start, size)]
        return pltpu.make_async_remote_copy(
            src_ref=rows, dst_ref=rows, send_sem=len_send.at[index], recv_sem=len_recv.at[index],
            device_id=(to, me), device_id_type=MESH,
        )

    lane = lax.broadcasted_iota(jnp.int32, (BLOCK, HEAD), 1)
    row = lax.broadcasted_iota(jnp.int32, (BLOCK, HEAD), 0)
    pair = jnp.where(lane < HALF_TURN, lane, lane - HALF_TURN).astype(jnp.float32)
    frequency = jnp.exp(-math.log(ROPE_BASE) * (2.0 * pair) / HEAD)
    sign = jnp.where(lane < HALF_TURN, -1.0, 1.0)
    angle = row.astype(jnp.float32) * frequency
    cos_row[...] = jnp.cos(angle)
    sin_row[...] = jnp.sin(angle) * sign

    blk_row = lax.broadcasted_iota(jnp.int32, (2 * SLOTS, HEAD), 0)
    blk_of = jnp.zeros((2 * SLOTS, HEAD), jnp.int32)
    for s in range(SLOTS):
        for half in range(2):
            blk_of = jnp.where(blk_row == 2 * s + half, table[0, s, half], blk_of)
    base = (blk_of * BLOCK).astype(jnp.float32) * frequency[: 2 * SLOTS]
    cos_blk[...] = jnp.cos(base)
    sin_blk[...] = jnp.sin(base) * sign[: 2 * SLOTS]

    def turn_tables(source, half):
        at = pl.ds(2 * source + half, 1)
        cos_b = jnp.broadcast_to(cos_blk[at, :], (BLOCK, HEAD))
        sin_b = jnp.broadcast_to(sin_blk[at, :], (BLOCK, HEAD))
        cos_r, sin_r = cos_row[...], sin_row[...]
        return cos_b * cos_r - sin_b * sin_r, sin_b * cos_r + cos_b * sin_r

    def rotated(part, cosine, sine):
        part = part.astype(jnp.float32)
        return part * cosine + pltpu.roll(part, HALF_TURN, 1) * sine

    residue = []
    for h in range(HEAD_DIVISIONS):
        wanted = slot * HEAD_DIVISIONS + h
        found = jnp.int32(0)
        for r in range(RESIDUES):
            found = found + pick(rank_of[0, r] == wanted, r)
        residue.append(found)
    c_row = lax.broadcasted_iota(jnp.int32, (64, 2 * BLOCK), 0)
    c_col = lax.broadcasted_iota(jnp.int32, (64, 2 * BLOCK), 1)
    wanted_col = ((c_row % 16) // 8) * BLOCK + (c_row % 8) * RESIDUES
    for h in range(HEAD_DIVISIONS):
        wanted_col = wanted_col + pick(c_row // 16 == h, residue[h])
    choose[...] = jnp.where(c_col == wanted_col, 1.0, 0.0).astype(jnp.bfloat16)

    mate_copy = len_copy(0, req, 1, mate)
    mate_copy.start()
    sent.append(mate_copy)

    for load in loads:
        load.wait()

    for half in range(2):
        cosine, sine = turn_tables(slot, half)
        for head in range(2 * KV_DEV):
            part = q_raw[half * BLOCK : (half + 1) * BLOCK, head * HEAD : (head + 1) * HEAD]
            turned = rotated(part, cosine, sine) * QUERY_SCALE
            qrot[head // 2, (head % 2) * 2 + half] = turned.astype(jnp.bfloat16)
    num[...] = jnp.zeros_like(num)
    den[...] = jnp.zeros_like(den)

    q_block = [table[0, slot, half] for half in range(2)]
    tile_row = lax.broadcasted_iota(jnp.int32, (BLOCK, BLOCK), 0)
    tile_col = lax.broadcasted_iota(jnp.int32, (BLOCK, BLOCK), 1)

    def prepare(order):
        j = ORDER[order]
        source = (slot + SLOTS - j) % SLOTS
        for half in range(2):
            cosine, sine = turn_tables(source, half)
            for head in range(KV_DEV):
                part = kbuf[j, half * BLOCK : (half + 1) * BLOCK, head * HEAD : (head + 1) * HEAD]
                krot[head, half * BLOCK : (half + 1) * BLOCK, :] = rotated(part, cosine, sine).astype(
                    jnp.bfloat16
                )
        for head in range(KV_DEV):
            for kind in range(2):
                cols = slice(head * HEAD, (head + 1) * HEAD)
                data = krot[head] if kind == 0 else vbuf[j, :, cols]
                rows = jnp.dot(choose[...], data, preferred_element_type=jnp.float32)
                rows = rows.astype(jnp.bfloat16)
                first = kind * KV_DEV * HEAD + head * HEAD
                for h in range(HEAD_DIVISIONS):
                    chosen[h, order, :, first : first + HEAD] = rows[h * 16 : (h + 1) * 16]

    def attend(order, head):
        j = ORDER[order]
        source = (slot + SLOTS - j) % SLOTS
        for half in range(2):
            k_block = table[0, source, half]

            def tile(t, carry):
                k_part = krot[head, half * BLOCK : (half + 1) * BLOCK, :]
                v_part = vbuf[j, half * BLOCK : (half + 1) * BLOCK, head * HEAD : (head + 1) * HEAD]
                q_block_now = jnp.where(t % 2 == 0, q_block[0], q_block[1])
                scores = lax.dot_general(
                    qrot[head, t], k_part, (((1,), (1,)), ((), ())),
                    preferred_element_type=jnp.float32,
                )
                expo = jnp.exp(CAP * jnp.tanh(scores * (1.0 / CAP)))
                behind = (q_block_now - k_block) * BLOCK
                expo = jnp.where(tile_col - tile_row <= behind, expo, 0.0)
                den[head, t] += expo[:, :HEAD] + expo[:, HEAD:]
                num[head, t] += jnp.dot(
                    expo.astype(jnp.bfloat16), v_part, preferred_element_type=jnp.float32
                )
                return carry

            lax.fori_loop(0, 4, tile, 0)

    def share(batch, first, count):
        for e in (1, 2, 3):
            peer = quad_peer(e)
            copy = pltpu.make_async_remote_copy(
                src_ref=chosen.at[peer, pl.ds(first, count)],
                dst_ref=arrived.at[e, pl.ds(first, count)],
                send_sem=pick_send.at[e, batch],
                recv_sem=pick_recv.at[e, batch],
                device_id=(req, slot * HEAD_DIVISIONS + peer),
                device_id_type=MESH,
            )
            copy.start()
            sent.append(copy)
            shares.append(copy)

    shares = []

    prepare(0)
    for head in range(KV_DEV):
        attend(0, head)

    len_waits = [mate_copy]
    for turn in range(1, 5):
        for chunk in range(4):
            for side in range(2):
                if turn == 4 and chunk // 2 != side:
                    continue
                hop(side, turn - 1, chunk).wait_recv()
                if travels(side, turn, chunk):
                    copy = hop(side, turn, chunk)
                    copy.start()
                    sent.append(copy)
        if turn == 1:
            mate_copy.wait_recv()
            y_copy = len_copy(1, (req // 2) * 2, 2, y_mate)
            y_copy.start()
            sent.append(y_copy)
        if turn == 2:
            y_copy.wait_recv()
            x_copies = [len_copy(2 + i, (req // 4) * 4, 4, x_mates[i]) for i in range(3)]
            for copy in x_copies:
                copy.start()
                sent.append(copy)
        if turn == 3:
            share(0, 0, 5)
        if turn < 4:
            for order in (2 * turn - 1, 2 * turn):
                prepare(order)
                for head in range(KV_DEV):
                    attend(order, head)
        else:
            share(1, 5, 2)
            prepare(7)
            attend(7, 0)
            share(2, 7, 1)
            attend(7, 1)

    for copy in x_copies:
        copy.wait_recv()
    length = jnp.zeros((8, 128), jnp.int32)
    for p in range(16):
        length = length + pick(group_of[p] == req, lens[p])
    length = length[0:1, :]

    for half in range(2):
        rows = slice(half * BLOCK, (half + 1) * BLOCK)
        live = row + q_block[half] * BLOCK < jnp.broadcast_to(length, (BLOCK, HEAD))
        for head in range(2 * KV_DEV):
            total = jnp.sum(den[head // 2, (head % 2) * 2 + half], axis=1, keepdims=True)
            value = num[head // 2, (head % 2) * 2 + half] / total
            out_ref[rows, head * HEAD : (head + 1) * HEAD] = jnp.where(live, value, 0.0).astype(jnp.bfloat16)

    own_residue = jnp.int32(0)
    for r in range(RESIDUES):
        own_residue = own_residue + pick(rank_of[0, r] == me, r)
    p_row = lax.broadcasted_iota(jnp.int32, (HEAD, HEAD), 0)
    p_col = lax.broadcasted_iota(jnp.int32, (HEAD, HEAD), 1)
    place = p_col % 8
    for order in range(8):
        source = (slot + SLOTS - ORDER[order]) % SLOTS
        for half in range(2):
            place = place + pick(p_col // 8 == 2 * order + half, table[0, source, half] * 8)
    kept = p_row * RESIDUES + own_residue < jnp.broadcast_to(length, (HEAD, HEAD))
    placed = jnp.where(jnp.logical_and(place == p_row, kept), 1.0, 0.0).astype(jnp.bfloat16)

    for copy in shares:
        copy.wait_recv()
    width = KV_DEV * HEAD
    for e in range(4):
        from_head = head_group if e == 0 else quad_peer(e)
        data = chosen[head_group] if e == 0 else arrived[e]
        data = data.reshape(8 * 16, 2 * width)
        moved = jnp.dot(placed, data, preferred_element_type=jnp.float32).astype(jnp.bfloat16)
        for kind in range(2):
            start = pl.multiple_of(kind * HEAD_DIVISIONS * width + from_head * width, width)
            cache_ref[:, pl.ds(start, width)] = moved[:, kind * width : (kind + 1) * width]

    for copy in sent:
        copy.wait_send()


def on_device(queries, keys, values, block_map, lengths, group_of_prompt, decode_rank):
    rows = queries.shape[2]
    wide, narrow = queries.shape[3], keys.shape[3]
    anywhere = pl.BlockSpec(memory_space=pl.ANY)
    scalars = pl.BlockSpec(memory_space=pltpu.SMEM)
    vmem = pl.BlockSpec(memory_space=pltpu.VMEM)
    dma = pltpu.SemaphoreType.DMA
    bf16, f32 = jnp.bfloat16, jnp.float32
    out, cache = pl.pallas_call(
        kernel,
        out_shape=(
            jax.ShapeDtypeStruct((rows, wide), bf16),
            jax.ShapeDtypeStruct((rows // HEAD_DIVISIONS, 2048), bf16),
        ),
        in_specs=[anywhere] * 3 + [scalars] * 4,
        out_specs=(vmem, vmem),
        scratch_shapes=[
            pltpu.VMEM((rows, wide), bf16),
            pltpu.VMEM((SLOTS, rows, narrow), bf16),
            pltpu.VMEM((SLOTS, rows, narrow), bf16),
            pltpu.VMEM((KV_DEV, 4, BLOCK, HEAD), bf16),
            pltpu.VMEM((KV_DEV, rows, HEAD), bf16),
            pltpu.VMEM((KV_DEV, 4, BLOCK, HEAD), f32),
            pltpu.VMEM((KV_DEV, 4, BLOCK, HEAD), f32),
            pltpu.VMEM((BLOCK, HEAD), f32),
            pltpu.VMEM((BLOCK, HEAD), f32),
            pltpu.VMEM((2 * SLOTS, HEAD), f32),
            pltpu.VMEM((2 * SLOTS, HEAD), f32),
            pltpu.VMEM((64, 2 * BLOCK), bf16),
            pltpu.VMEM((HEAD_DIVISIONS, SLOTS, 16, 2 * narrow), bf16),
            pltpu.VMEM((HEAD_DIVISIONS, SLOTS, 16, 2 * narrow), bf16),
            pltpu.VMEM((16, 8, 128), jnp.int32),
            dma((3,)),
            dma((2, 4, 4)),
            dma((SLOTS, 4)),
            dma((4, 3)),
            dma((4, 3)),
            dma((5,)),
            dma((5,)),
        ],
        compiler_params=pltpu.CompilerParams(collective_id=0, has_side_effects=True),
    )(
        queries.reshape(rows, wide), keys.reshape(rows, narrow), values.reshape(rows, narrow),
        block_map, lengths, group_of_prompt, decode_rank,
    )
    return out[None, None], cache[None]


def solution(mesh):
    placed = (
        P("req", "blk", None, None),
        P("req", "blk", None, None),
        P("req", "blk", None, None),
        P("req", None, None),
        P("req"),
        P(),
        P("req", None),
    )
    return jax.shard_map(
        on_device,
        mesh=mesh,
        in_specs=placed,
        out_specs=(P("req", "blk", None, None), P("req", "blk", None)),
        check_vma=False,
    )
```

time: 277 us -> 117 us (0.42)
  the two profiles are of different devices: /device:TPU:16 before, /device:TPU:1 now
where the time goes in v1:
time: 117 us
  Pallas kernels  111 us (95%)
  local copies, waits for them, and re-layouts  4.07 us (3%)
  between operations  1.3 us (1%)
    pallas_call x1, Pallas kernels, on_device(): pl.pallas_call(kernel, out_shape=(jax.ShapeDtypeStruct((rows, wide), bf16...  111 us
    unnamed x7, local copies, waits for them, and re-layouts  4.07 us

profile of v1, /device:TPU:1, one launch (start us, length us, event | category | flops | bytes accessed | tf_op | source)
XLA Modules:
  0.0 116.5 jit_solution(10258105103567294519)
XLA Ops:
  1.3 0.0 copy-start.1
  1.3 0.7 copy-done.1
  2.0 0.7 copy.9.table
  2.6 111.2 %shard_map.86 = (bf16[512,512]{1,0:T(8,128)(2,1)}, bf16[128,2048]{1,0:T(8,128)(2,1)}) custom-call(bf16[512,512]{1,0:T(8,128)(2,1)} %bitcast.5, bf16[512,256]{1,0:T(8,128)(2,1)} %bitcast.8, bf16[512,256]{1,0:T(8,128)(2,1)} %bitcast.9, s32[1,8,2]{2,1,0:T(8,128)} %copy.9.table, s32[1]{0:T(128)S(6)} %copy.12.length_ref, s32[16]{0:T(128)} %group_of.1, ...), custom_call_target="tpu_custom_call" | custom-call | tf_op jit(solution)/shard_map/pallas_call | solution.py:336
  113.8 0.0 copy-start
  113.8 1.9 %copy.13 = bf16[1,1,512,512]{3,2,1,0:T(8,128)(2,1)} copy(bf16[1,1,512,512]{3,2,1,0:T(8,128)(2,1)} %bitcast.7) | data formatting | bytes 1048576
  115.7 0.0 copy-done
  115.7 0.8 copy.14
Async XLA Ops:
  1.3 0.7 copy-start.1
  113.8 1.9 %copy-start = (bf16[128,2048]{1,0:T(8,128)(2,1)S(1)}, bf16[128,2048]{1,0:T(8,128)(2,1)}, u32[]{:S(2)}) copy-start(bf16[128,2048]{1,0:T(8,128)(2,1)} %get-tuple-element.5) | copy-start | bytes 1572868

commit v2 on v1

--- a/solution.py
+++ b/solution.py
@@ -30,7 +30,7 @@
     q_hbm, k_hbm, v_hbm, table, length_ref, group_of, rank_of,
     out_ref, cache_ref,
     q_raw, kbuf, vbuf, qrot, krot, num, den, cos_row, sin_row, cos_blk, sin_blk,
-    choose, chosen, arrived, lens,
+    choose, chosen, arrived, lens, kpair, vpair, kept_weight,
     load_sem, send_sem, recv_sem, pick_send, pick_recv, len_send, len_recv,
 ):
     req = lax.axis_index("req")
@@ -129,7 +129,7 @@
     blk_of = jnp.zeros((2 * SLOTS, HEAD), jnp.int32)
     for s in range(SLOTS):
         for half in range(2):
-            blk_of = jnp.where(blk_row == 2 * s + half, table[0, s, half], blk_of)
+            blk_of = jnp.where(blk_row == 2 * s + half, table[0, half, s], blk_of)
     base = (blk_of * BLOCK).astype(jnp.float32) * frequency[: 2 * SLOTS]
     cos_blk[...] = jnp.cos(base)
     sin_blk[...] = jnp.sin(base) * sign[: 2 * SLOTS]
@@ -166,63 +166,140 @@
     for load in loads:
         load.wait()
 
-    for half in range(2):
-        cosine, sine = turn_tables(slot, half)
-        for head in range(2 * KV_DEV):
-            part = q_raw[half * BLOCK : (half + 1) * BLOCK, head * HEAD : (head + 1) * HEAD]
-            turned = rotated(part, cosine, sine) * QUERY_SCALE
-            qrot[head // 2, (head % 2) * 2 + half] = turned.astype(jnp.bfloat16)
+    q_block = [table[0, half, slot] for half in range(2)]
+    own_low = jnp.minimum(q_block[0], q_block[1])
+    first_low = q_block[0] < q_block[1]
+    q_tables = [turn_tables(slot, half) for half in range(2)]
+    for head in range(2 * KV_DEV):
+        cols = slice(head * HEAD, (head + 1) * HEAD)
+        turned = [rotated(q_raw[h * BLOCK : (h + 1) * BLOCK, cols], *q_tables[h]) * QUERY_SCALE for h in range(2)]
+        at = (head % 2) * 2
+        qrot[head // 2, at] = jnp.where(first_low, turned[0], turned[1]).astype(jnp.bfloat16)
+        qrot[head // 2, at + 1] = jnp.where(first_low, turned[1], turned[0]).astype(jnp.bfloat16)
     num[...] = jnp.zeros_like(num)
     den[...] = jnp.zeros_like(den)
 
-    q_block = [table[0, slot, half] for half in range(2)]
     tile_row = lax.broadcasted_iota(jnp.int32, (BLOCK, BLOCK), 0)
     tile_col = lax.broadcasted_iota(jnp.int32, (BLOCK, BLOCK), 1)
 
-    def prepare(order):
+    def choose_rows(order, kind, load):
+        for head in range(KV_DEV):
+            rows = jnp.dot(choose[...], load(head), preferred_element_type=jnp.float32)
+            rows = rows.astype(jnp.bfloat16)
+            first = kind * KV_DEV * HEAD + head * HEAD
+            for h in range(HEAD_DIVISIONS):
+                chosen[h, order, :, first : first + HEAD] = rows[h * 16 : (h + 1) * 16]
+
+    def prepare_keys(order):
         j = ORDER[order]
         source = (slot + SLOTS - j) % SLOTS
         for half in range(2):
             cosine, sine = turn_tables(source, half)
+            rows = slice(half * BLOCK, (half + 1) * BLOCK)
             for head in range(KV_DEV):
-                part = kbuf[j, half * BLOCK : (half + 1) * BLOCK, head * HEAD : (head + 1) * HEAD]
-                krot[head, half * BLOCK : (half + 1) * BLOCK, :] = rotated(part, cosine, sine).astype(
-                    jnp.bfloat16
-                )
+                part = kbuf[j, rows, head * HEAD : (head + 1) * HEAD]
+                krot[head, rows, :] = rotated(part, cosine, sine).astype(jnp.bfloat16)
+        choose_rows(order, 0, lambda head: krot[head])
+        place(order, lambda head, half: krot[head, half * BLOCK : (half + 1) * BLOCK, :], kpair)
+
+    def prepare_values(order):
+        j = ORDER[order]
+
+        def rows_of(head, half):
+            return vbuf[j, half * BLOCK : (half + 1) * BLOCK, head * HEAD : (head + 1) * HEAD]
+
+        choose_rows(order, 1, lambda head: vbuf[j, :, head * HEAD : (head + 1) * HEAD])
+        place(order, rows_of, vpair)
+
+    def prepare(order):
+        prepare_keys(order)
+        prepare_values(order)
+
+    def meeting(order):
+        source = (slot + SLOTS - ORDER[order]) % SLOTS
+        first, second = table[0, 0, source], table[0, 1, source]
+        to_low = jnp.minimum(first, second) < own_low
+        low_first = jnp.where(first < second, 1, 0)
+        other_first = jnp.where(to_low, low_first, 1 - low_first)
+        return low_first == 1, other_first == 1, to_low
+
+    def place(order, rows_of, target):
+        low_first, other_first, _ = meeting(order)
+        if order == 0:
+            other_first = jnp.logical_not(low_first)
         for head in range(KV_DEV):
-            for kind in range(2):
-                cols = slice(head * HEAD, (head + 1) * HEAD)
-                data = krot[head] if kind == 0 else vbuf[j, :, cols]
-                rows = jnp.dot(choose[...], data, preferred_element_type=jnp.float32)
-                rows = rows.astype(jnp.bfloat16)
-                first = kind * KV_DEV * HEAD + head * HEAD
-                for h in range(HEAD_DIVISIONS):
-                    chosen[h, order, :, first : first + HEAD] = rows[h * 16 : (h + 1) * 16]
+            first, second = rows_of(head, 0), rows_of(head, 1)
+            target[head, 0] = jnp.where(low_first, first, second)
+            target[head, 1] = jnp.where(other_first, first, second)
+
+    def weigh(q_part, k_part, masked=False):
+        scores = lax.dot_general(
+            q_part, k_part, (((1,), (1,)), ((), ())), preferred_element_type=jnp.float32
+        )
+        expo = jnp.exp(CAP * jnp.tanh(scores * (1.0 / CAP)))
+        if masked:
+            expo = jnp.where(tile_col <= tile_row, expo, 0.0)
+        return expo.astype(jnp.bfloat16), expo[:, :HEAD] + expo[:, HEAD:]
+
+    def blend(weight, v_part):
+        return jnp.dot(weight, v_part, preferred_element_type=jnp.float32)
+
+    def attend_own(head):
+        def tile(g, carry):
+            weight, part = weigh(qrot[head, 2 * g], kpair[head, 0], True)
+            num[head, 2 * g] = blend(weight, vpair[head, 0])
+            den[head, 2 * g] = part
+            weight, part = weigh(qrot[head, 2 * g + 1], kpair[head, 0])
+            weight2, part2 = weigh(qrot[head, 2 * g + 1], kpair[head, 1], True)
+            num[head, 2 * g + 1] = blend(weight, vpair[head, 0]) + blend(weight2, vpair[head, 1])
+            den[head, 2 * g + 1] = part + part2
+            return carry
+
+        lax.fori_loop(0, 2, tile, 0)
+
+    def add_parts(total, head, g, to_low, always, either):
+        total[head, 2 * g] += jnp.where(to_low, either, 0.0)
+        total[head, 2 * g + 1] += always + jnp.where(to_low, 0.0, either)
 
     def attend(order, head):
-        j = ORDER[order]
-        source = (slot + SLOTS - j) % SLOTS
-        for half in range(2):
-            k_block = table[0, source, half]
-
-            def tile(t, carry):
-                k_part = krot[head, half * BLOCK : (half + 1) * BLOCK, :]
-                v_part = vbuf[j, half * BLOCK : (half + 1) * BLOCK, head * HEAD : (head + 1) * HEAD]
-                q_block_now = jnp.where(t % 2 == 0, q_block[0], q_block[1])
-                scores = lax.dot_general(
-                    qrot[head, t], k_part, (((1,), (1,)), ((), ())),
-                    preferred_element_type=jnp.float32,
-                )
-                expo = jnp.exp(CAP * jnp.tanh(scores * (1.0 / CAP)))
-                behind = (q_block_now - k_block) * BLOCK
-                expo = jnp.where(tile_col - tile_row <= behind, expo, 0.0)
-                den[head, t] += expo[:, :HEAD] + expo[:, HEAD:]
-                num[head, t] += jnp.dot(
-                    expo.astype(jnp.bfloat16), v_part, preferred_element_type=jnp.float32
-                )
-                return carry
-
-            lax.fori_loop(0, 4, tile, 0)
+        _, _, to_low = meeting(order)
+
+        def tile(g, carry):
+            lower, upper = qrot[head, 2 * g], qrot[head, 2 * g + 1]
+            weight, part = weigh(upper, kpair[head, 0])
+            weight2, part2 = weigh(jnp.where(to_low, lower, upper), kpair[head, 1])
+            add_parts(den, head, g, to_low, part, part2)
+            always = blend(weight, vpair[head, 0])
+            either = blend(weight2, vpair[head, 1])
+            add_parts(num, head, g, to_low, always, either)
+            return carry
+
+        lax.fori_loop(0, 2, tile, 0)
+
+    def weigh_last(order, head):
+        _, _, to_low = meeting(order)
+
+        def tile(g, carry):
+            lower, upper = qrot[head, 2 * g], qrot[head, 2 * g + 1]
+            weight, part = weigh(upper, kpair[head, 0])
+            weight2, part2 = weigh(jnp.where(to_low, lower, upper), kpair[head, 1])
+            kept_weight[head, 2 * g] = weight
+            kept_weight[head, 2 * g + 1] = weight2
+            add_parts(den, head, g, to_low, part, part2)
+            return carry
+
+        lax.fori_loop(0, 2, tile, 0)
+
+    def blend_last(order, head):
+        _, _, to_low = meeting(order)
+
+        def tile(g, carry):
+            always = blend(kept_weight[head, 2 * g], vpair[head, 0])
+            either = blend(kept_weight[head, 2 * g + 1], vpair[head, 1])
+            add_parts(num, head, g, to_low, always, either)
+            return carry
+
+        lax.fori_loop(0, 2, tile, 0)
 
     def share(batch, first, count):
         for e in (1, 2, 3):
@@ -241,45 +318,59 @@
 
     shares = []
 
-    prepare(0)
-    for head in range(KV_DEV):
-        attend(0, head)
-
-    len_waits = [mate_copy]
-    for turn in range(1, 5):
+    def own_keys_and_first():
+        prepare(0)
+        attend_own(0)
+
+    def first_of(order):
+        prepare(order)
+        attend(order, 0)
+
+    work = {
+        1: [own_keys_and_first, lambda: attend_own(1), lambda: None, lambda: None],
+        2: [lambda: first_of(1), lambda: attend(1, 1), lambda: first_of(2), lambda: attend(2, 1)],
+        3: [lambda: first_of(3), lambda: attend(3, 1), lambda: first_of(4), lambda: attend(4, 1)],
+    }
+    for turn in range(1, 4):
         for chunk in range(4):
             for side in range(2):
-                if turn == 4 and chunk // 2 != side:
-                    continue
                 hop(side, turn - 1, chunk).wait_recv()
                 if travels(side, turn, chunk):
                     copy = hop(side, turn, chunk)
                     copy.start()
                     sent.append(copy)
-        if turn == 1:
-            mate_copy.wait_recv()
-            y_copy = len_copy(1, (req // 2) * 2, 2, y_mate)
-            y_copy.start()
-            sent.append(y_copy)
-        if turn == 2:
-            y_copy.wait_recv()
-            x_copies = [len_copy(2 + i, (req // 4) * 4, 4, x_mates[i]) for i in range(3)]
-            for copy in x_copies:
-                copy.start()
-                sent.append(copy)
-        if turn == 3:
-            share(0, 0, 5)
-        if turn < 4:
-            for order in (2 * turn - 1, 2 * turn):
-                prepare(order)
-                for head in range(KV_DEV):
-                    attend(order, head)
-        else:
-            share(1, 5, 2)
-            prepare(7)
-            attend(7, 0)
-            share(2, 7, 1)
-            attend(7, 1)
+            if chunk == 0 and turn == 2:
+                mate_copy.wait_recv()
+                y_copy = len_copy(1, (req // 2) * 2, 2, y_mate)
+                y_copy.start()
+                sent.append(y_copy)
+            if chunk == 0 and turn == 3:
+                y_copy.wait_recv()
+                x_copies = [len_copy(2 + i, (req // 4) * 4, 4, x_mates[i]) for i in range(3)]
+                for copy in x_copies:
+                    copy.start()
+                    sent.append(copy)
+                share(0, 0, 3)
+            work[turn][chunk]()
+    share(1, 3, 2)
+    prepare(5)
+    attend(5, 0)
+    attend(5, 1)
+    prepare(6)
+    attend(6, 0)
+    attend(6, 1)
+    share(2, 5, 2)
+    hop(0, 3, 0).wait_recv()
+    hop(1, 3, 2).wait_recv()
+    prepare_keys(7)
+    weigh_last(7, 0)
+    weigh_last(7, 1)
+    hop(0, 3, 1).wait_recv()
+    hop(1, 3, 3).wait_recv()
+    prepare_values(7)
+    blend_last(7, 0)
+    share(3, 7, 1)
+    blend_last(7, 1)
 
     for copy in x_copies:
         copy.wait_recv()
@@ -291,9 +382,12 @@
     for half in range(2):
         rows = slice(half * BLOCK, (half + 1) * BLOCK)
         live = row + q_block[half] * BLOCK < jnp.broadcast_to(length, (BLOCK, HEAD))
+        lower_here = first_low if half == 0 else jnp.logical_not(first_low)
         for head in range(2 * KV_DEV):
-            total = jnp.sum(den[head // 2, (head % 2) * 2 + half], axis=1, keepdims=True)
-            value = num[head // 2, (head % 2) * 2 + half] / total
+            at = (head % 2) * 2
+            parts = jnp.where(lower_here, den[head // 2, at], den[head // 2, at + 1])
+            total = jnp.sum(parts, axis=1, keepdims=True)
+            value = jnp.where(lower_here, num[head // 2, at], num[head // 2, at + 1]) / total
             out_ref[rows, head * HEAD : (head + 1) * HEAD] = jnp.where(live, value, 0.0).astype(jnp.bfloat16)
 
     own_residue = jnp.int32(0)
@@ -305,7 +399,7 @@
     for order in range(8):
         source = (slot + SLOTS - ORDER[order]) % SLOTS
         for half in range(2):
-            place = place + pick(p_col // 8 == 2 * order + half, table[0, source, half] * 8)
+            place = place + pick(p_col // 8 == 2 * order + half, table[0, half, source] * 8)
     kept = p_row * RESIDUES + own_residue < jnp.broadcast_to(length, (HEAD, HEAD))
     placed = jnp.where(jnp.logical_and(place == p_row, kept), 1.0, 0.0).astype(jnp.bfloat16)
 
@@ -328,7 +422,7 @@
 def on_device(queries, keys, values, block_map, lengths, group_of_prompt, decode_rank):
     rows = queries.shape[2]
     wide, narrow = queries.shape[3], keys.shape[3]
-    anywhere = pl.BlockSpec(memory_space=pl.ANY)
+    anywhere = pl.BlockSpec(memory_space=pltpu.HBM)
     scalars = pl.BlockSpec(memory_space=pltpu.SMEM)
     vmem = pl.BlockSpec(memory_space=pltpu.VMEM)
     dma = pltpu.SemaphoreType.DMA
@@ -357,18 +451,25 @@
             pltpu.VMEM((HEAD_DIVISIONS, SLOTS, 16, 2 * narrow), bf16),
             pltpu.VMEM((HEAD_DIVISIONS, SLOTS, 16, 2 * narrow), bf16),
             pltpu.VMEM((16, 8, 128), jnp.int32),
+            pltpu.VMEM((KV_DEV, 2, BLOCK, HEAD), bf16),
+            pltpu.VMEM((KV_DEV, 2, BLOCK, HEAD), bf16),
+            pltpu.VMEM((KV_DEV, 4, BLOCK, BLOCK), bf16),
             dma((3,)),
             dma((2, 4, 4)),
             dma((SLOTS, 4)),
-            dma((4, 3)),
-            dma((4, 3)),
+            dma((4, 4)),
+            dma((4, 4)),
             dma((5,)),
             dma((5,)),
         ],
-        compiler_params=pltpu.CompilerParams(collective_id=0, has_side_effects=True),
+        compiler_params=pltpu.CompilerParams(collective_id=0, has_side_effects=True, vmem_limit_bytes=32 * 2**20),
     )(
-        queries.reshape(rows, wide), keys.reshape(rows, narrow), values.reshape(rows, narrow),
-        block_map, lengths, group_of_prompt, decode_rank,
+        *[pltpu.with_memory_space_constraint(a, pltpu.HBM) for a in (
+            queries.reshape(rows, wide), keys.reshape(rows, narrow), values.reshape(rows, narrow),
+            jnp.swapaxes(block_map, 1, 2),
+        )],
+        lengths,
+        *[pltpu.with_memory_space_constraint(a, pltpu.HBM) for a in (group_of_prompt, decode_rank)],
     )
     return out[None, None], cache[None]
 

time: 117 us -> 106 us (0.906)
  Pallas kernels: 111 us -> 103 us
  local copies, waits for them, and re-layouts: 4.07 us -> 1.59 us
    pallas_call x1, Pallas kernels: 111 us -> 103 us  [on_device(): pl.pallas_call(kernel, out_shape=(jax.ShapeDtypeStruct((rows, wide), bf16...]
    unnamed x7 -> x2, local copies, waits for them, and re-layouts: 4.07 us -> 1.59 us
where the time goes in v2:
time: 106 us
  Pallas kernels  103 us (97%)
  local copies, waits for them, and re-layouts  1.59 us (2%)
  between operations  1.29 us (1%)
    pallas_call x1, Pallas kernels, on_device(): pl.pallas_call(kernel, out_shape=(jax.ShapeDtypeStruct((rows, wide), bf16...  103 us

profile of v2, /device:TPU:1, one launch (start us, length us, event | category | flops | bytes accessed | tf_op | source)
XLA Modules:
  0.0 105.6 jit_solution(16397569274917297826)
XLA Ops:
  1.3 102.7 %shard_map.86 = (bf16[512,512]{1,0:T(8,128)(2,1)S(1)}, bf16[128,2048]{1,0:T(8,128)(2,1)S(1)}) custom-call(bf16[512,512]{1,0:T(8,128)(2,1)} %bitcast.8, bf16[512,256]{1,0:T(8,128)(2,1)} %bitcast.9, bf16[512,256]{1,0:T(8,128)(2,1)} %bitcast.10, s32[1,2,8]{2,1,0:T(2,128)} %bitcast.11, s32[1]{0:T(128)S(6)} %copy.11.length_ref, s32[16]{0:T(128)} %group_of.1, ...), custom_call_target="tpu_custom_call" | custom-call | tf_op jit(solution)/shard_map/pallas_call | solution.py:430
  104.0 0.8 copy.12
  104.8 0.8 copy.13

commit v3 on v2

--- a/solution.py
+++ b/solution.py
@@ -50,6 +50,9 @@
             high = 1 - high
         return high * 2 + low
 
+    parity = head_group // 2
+    across = (slot + SLOTS - 1 + 2 * parity) % SLOTS
+
     core = req % 2
     y_low = (req // 2) % 2
     x = req // 4
@@ -68,6 +71,7 @@
     barrier = pltpu.get_barrier_semaphore()
     partners = [(req, right), (req, left)]
     partners += [(req, slot * HEAD_DIVISIONS + quad_peer(e)) for e in (1, 2, 3)]
+    partners += [(req, across * HEAD_DIVISIONS + quad_peer(e)) for e in (2, 3)]
     partners += [(mate, me), (y_mate, me)] + [(xm, me) for xm in x_mates]
     for partner in partners:
         pl.semaphore_signal(barrier, inc=1, device_id=partner, device_id_type=MESH)
@@ -101,9 +105,9 @@
         return turn == 3 and (chunk // 2 == side)
 
     sent = []
-    for chunk in range(4):
+    for place_in_line in range(4):
         for side in range(2):
-            copy = hop(side, 0, chunk)
+            copy = hop(side, 0, (place_in_line + 2 * side) % 4)
             copy.start()
             sent.append(copy)
 
@@ -145,18 +149,19 @@
         part = part.astype(jnp.float32)
         return part * cosine + pltpu.roll(part, HALF_TURN, 1) * sine
 
+    peers = [slot * HEAD_DIVISIONS + (head_group if e == 0 else quad_peer(e)) for e in range(4)]
+    peers += [across * HEAD_DIVISIONS + quad_peer(e) for e in (2, 3)]
     residue = []
-    for h in range(HEAD_DIVISIONS):
-        wanted = slot * HEAD_DIVISIONS + h
+    for wanted in peers:
         found = jnp.int32(0)
         for r in range(RESIDUES):
             found = found + pick(rank_of[0, r] == wanted, r)
         residue.append(found)
-    c_row = lax.broadcasted_iota(jnp.int32, (64, 2 * BLOCK), 0)
-    c_col = lax.broadcasted_iota(jnp.int32, (64, 2 * BLOCK), 1)
+    c_row = lax.broadcasted_iota(jnp.int32, (16 * len(peers), 2 * BLOCK), 0)
+    c_col = lax.broadcasted_iota(jnp.int32, (16 * len(peers), 2 * BLOCK), 1)
     wanted_col = ((c_row % 16) // 8) * BLOCK + (c_row % 8) * RESIDUES
-    for h in range(HEAD_DIVISIONS):
-        wanted_col = wanted_col + pick(c_row // 16 == h, residue[h])
+    for d in range(len(peers)):
+        wanted_col = wanted_col + pick(c_row // 16 == d, residue[d])
     choose[...] = jnp.where(c_col == wanted_col, 1.0, 0.0).astype(jnp.bfloat16)
 
     mate_copy = len_copy(0, req, 1, mate)
@@ -182,13 +187,16 @@
     tile_row = lax.broadcasted_iota(jnp.int32, (BLOCK, BLOCK), 0)
     tile_col = lax.broadcasted_iota(jnp.int32, (BLOCK, BLOCK), 1)
 
+    def shelf(j):
+        return (j + 2) % SLOTS
+
     def choose_rows(order, kind, load):
         for head in range(KV_DEV):
             rows = jnp.dot(choose[...], load(head), preferred_element_type=jnp.float32)
             rows = rows.astype(jnp.bfloat16)
             first = kind * KV_DEV * HEAD + head * HEAD
-            for h in range(HEAD_DIVISIONS):
-                chosen[h, order, :, first : first + HEAD] = rows[h * 16 : (h + 1) * 16]
+            for d in range(6):
+                chosen[d, shelf(ORDER[order]), :, first : first + HEAD] = rows[d * 16 : (d + 1) * 16]
 
     def prepare_keys(order):
         j = ORDER[order]
@@ -301,20 +309,19 @@
 
         lax.fori_loop(0, 2, tile, 0)
 
-    def share(batch, first, count):
-        for e in (1, 2, 3):
-            peer = quad_peer(e)
-            copy = pltpu.make_async_remote_copy(
-                src_ref=chosen.at[peer, pl.ds(first, count)],
-                dst_ref=arrived.at[e, pl.ds(first, count)],
-                send_sem=pick_send.at[e, batch],
-                recv_sem=pick_recv.at[e, batch],
-                device_id=(req, slot * HEAD_DIVISIONS + peer),
-                device_id_type=MESH,
-            )
-            copy.start()
-            sent.append(copy)
-            shares.append(copy)
+    def share(to, e, source_at, target_at, count):
+        index = len(shares)
+        copy = pltpu.make_async_remote_copy(
+            src_ref=chosen.at[e + 2 if to else e, pl.ds(source_at, count)],
+            dst_ref=arrived.at[e, pl.ds(target_at, count)],
+            send_sem=pick_send.at[index],
+            recv_sem=pick_recv.at[index],
+            device_id=(req, peers[e + 2 if to else e]),
+            device_id_type=MESH,
+        )
+        copy.start()
+        sent.append(copy)
+        shares.append(copy)
 
     shares = []
 
@@ -332,34 +339,41 @@
         3: [lambda: first_of(3), lambda: attend(3, 1), lambda: first_of(4), lambda: attend(4, 1)],
     }
     for turn in range(1, 4):
-        for chunk in range(4):
+        for place_in_line in range(4):
             for side in range(2):
+                chunk = (place_in_line + 2 * side) % 4
                 hop(side, turn - 1, chunk).wait_recv()
                 if travels(side, turn, chunk):
                     copy = hop(side, turn, chunk)
                     copy.start()
                     sent.append(copy)
-            if chunk == 0 and turn == 2:
+            if place_in_line == 0 and turn == 2:
                 mate_copy.wait_recv()
                 y_copy = len_copy(1, (req // 2) * 2, 2, y_mate)
                 y_copy.start()
                 sent.append(y_copy)
-            if chunk == 0 and turn == 3:
+            if place_in_line == 0 and turn == 3:
                 y_copy.wait_recv()
                 x_copies = [len_copy(2 + i, (req // 4) * 4, 4, x_mates[i]) for i in range(3)]
                 for copy in x_copies:
                     copy.start()
                     sent.append(copy)
-                share(0, 0, 3)
-            work[turn][chunk]()
-    share(1, 3, 2)
+            work[turn][place_in_line]()
+    share(0, 1, 0, 0, 5)
+    for e in (2, 3):
+        share(1, e, 2 - 2 * parity, 1, 2)
+        share(0, e, 0, 0, 1)
     prepare(5)
     attend(5, 0)
     attend(5, 1)
     prepare(6)
     attend(6, 0)
     attend(6, 1)
-    share(2, 5, 2)
+    for e in (1, 2, 3):
+        share(0, e, 5, 5, 1)
+        share(0, e, 7, 7, 1)
+    for e in (2, 3):
+        share(1, e, 4 - 2 * parity, 3, 2)
     hop(0, 3, 0).wait_recv()
     hop(1, 3, 2).wait_recv()
     prepare_keys(7)
@@ -369,7 +383,8 @@
     hop(1, 3, 3).wait_recv()
     prepare_values(7)
     blend_last(7, 0)
-    share(3, 7, 1)
+    for e in (1, 2, 3):
+        share(0, e, 6, 6, 1)
     blend_last(7, 1)
 
     for copy in x_copies:
@@ -399,7 +414,8 @@
     for order in range(8):
         source = (slot + SLOTS - ORDER[order]) % SLOTS
         for half in range(2):
-            place = place + pick(p_col // 8 == 2 * order + half, table[0, half, source] * 8)
+            here = p_col // 8 == 2 * shelf(ORDER[order]) + half
+            place = place + pick(here, table[0, half, source] * 8)
     kept = p_row * RESIDUES + own_residue < jnp.broadcast_to(length, (HEAD, HEAD))
     placed = jnp.where(jnp.logical_and(place == p_row, kept), 1.0, 0.0).astype(jnp.bfloat16)
 
@@ -408,7 +424,7 @@
     width = KV_DEV * HEAD
     for e in range(4):
         from_head = head_group if e == 0 else quad_peer(e)
-        data = chosen[head_group] if e == 0 else arrived[e]
+        data = chosen[0] if e == 0 else arrived[e]
         data = data.reshape(8 * 16, 2 * width)
         moved = jnp.dot(placed, data, preferred_element_type=jnp.float32).astype(jnp.bfloat16)
         for kind in range(2):
@@ -417,6 +433,15 @@
 
     for copy in sent:
         copy.wait_send()
+
+
+def put_out(out_ref, cache_ref, out_to, cache_to, sem):
+    first = pltpu.make_async_copy(out_ref, out_to, sem.at[0])
+    second = pltpu.make_async_copy(cache_ref, cache_to, sem.at[1])
+    first.start()
+    second.start()
+    first.wait()
+    second.wait()
 
 
 def on_device(queries, keys, values, block_map, lengths, group_of_prompt, decode_rank):
@@ -447,8 +472,8 @@
             pltpu.VMEM((BLOCK, HEAD), f32),
             pltpu.VMEM((2 * SLOTS, HEAD), f32),
             pltpu.VMEM((2 * SLOTS, HEAD), f32),
-            pltpu.VMEM((64, 2 * BLOCK), bf16),
-            pltpu.VMEM((HEAD_DIVISIONS, SLOTS, 16, 2 * narrow), bf16),
+            pltpu.VMEM((96, 2 * BLOCK), bf16),
+            pltpu.VMEM((6, SLOTS, 16, 2 * narrow), bf16),
             pltpu.VMEM((HEAD_DIVISIONS, SLOTS, 16, 2 * narrow), bf16),
             pltpu.VMEM((16, 8, 128), jnp.int32),
             pltpu.VMEM((KV_DEV, 2, BLOCK, HEAD), bf16),
@@ -457,8 +482,8 @@
             dma((3,)),
             dma((2, 4, 4)),
             dma((SLOTS, 4)),
-            dma((4, 4)),
-            dma((4, 4)),
+            dma((16,)),
+            dma((16,)),
             dma((5,)),
             dma((5,)),
         ],
@@ -471,6 +496,14 @@
         lengths,
         *[pltpu.with_memory_space_constraint(a, pltpu.HBM) for a in (group_of_prompt, decode_rank)],
     )
+    out, cache = pl.pallas_call(
+        put_out,
+        out_shape=(jax.ShapeDtypeStruct(out.shape, bf16), jax.ShapeDtypeStruct(cache.shape, bf16)),
+        in_specs=[pl.BlockSpec(memory_space=pltpu.VMEM)] * 2,
+        compiler_params=pltpu.CompilerParams(vmem_limit_bytes=8 * 2**20),
+        out_specs=(pl.BlockSpec(memory_space=pl.ANY),) * 2,
+        scratch_shapes=[dma((2,))],
+    )(out, cache)
     return out[None, None], cache[None]
 
 

time: 106 us -> 104 us (0.981)
  local copies, waits for them, and re-layouts: 1.59 us -> 0 us
    unnamed x2 -> x0, local copies, waits for them, and re-layouts: 1.59 us -> none
where the time goes in v3:
time: 104 us
  Pallas kernels  103 us (99%)
  between operations  1.29 us (1%)
    pallas_call x1, Pallas kernels, on_device(): pl.pallas_call(kernel, out_shape=(jax.ShapeDtypeStruct((rows, wide), bf16...  102 us

profile of v3, /device:TPU:1, one launch (start us, length us, event | category | flops | bytes accessed | tf_op | source)
XLA Modules:
  0.0 104.1 jit_solution(10925848894793811031)
XLA Ops:
  1.3 101.8 %shard_map.86 = (bf16[512,512]{1,0:T(8,128)(2,1)S(1)}, bf16[128,2048]{1,0:T(8,128)(2,1)S(1)}) custom-call(bf16[512,512]{1,0:T(8,128)(2,1)} %bitcast.6, bf16[512,256]{1,0:T(8,128)(2,1)} %bitcast.7, bf16[512,256]{1,0:T(8,128)(2,1)} %bitcast.8, s32[1,2,8]{2,1,0:T(2,128)} %bitcast.9, s32[1]{0:T(128)S(6)} %copy.9.length_ref, s32[16]{0:T(128)} %group_of.1, ...), custom_call_target="tpu_custom_call" | custom-call | tf_op jit(solution)/shard_map/pallas_call | solution.py:455
  103.1 1.0 shard_map.87

commit v4 on v3

--- a/solution.py
+++ b/solution.py
@@ -58,7 +58,7 @@
     x = req // 4
     mate = req + 1 - 2 * core
     y_mate = req + 2 - 4 * y_low
-    x_mates = [((x + i) % 4) * 4 + req % 4 for i in (1, 2, 3)]
+    x_mates = [(x + 1 - 2 * (x % 2)) * 4 + req % 4, ((x + 2) % 4) * 4 + req % 4]
 
     loads = [
         pltpu.make_async_copy(q_hbm, q_raw, load_sem.at[0]),
@@ -354,15 +354,18 @@
                 sent.append(y_copy)
             if place_in_line == 0 and turn == 3:
                 y_copy.wait_recv()
-                x_copies = [len_copy(2 + i, (req // 4) * 4, 4, x_mates[i]) for i in range(3)]
-                for copy in x_copies:
-                    copy.start()
-                    sent.append(copy)
+                x_copy = len_copy(2, (req // 4) * 4, 4, x_mates[0])
+                x_copy.start()
+                sent.append(x_copy)
             work[turn][place_in_line]()
     share(0, 1, 0, 0, 5)
     for e in (2, 3):
         share(1, e, 2 - 2 * parity, 1, 2)
         share(0, e, 0, 0, 1)
+    x_copy.wait_recv()
+    far_copy = len_copy(3, (req // 8) * 8, 8, x_mates[1])
+    far_copy.start()
+    sent.append(far_copy)
     prepare(5)
     attend(5, 0)
     attend(5, 1)
@@ -382,13 +385,12 @@
     hop(0, 3, 1).wait_recv()
     hop(1, 3, 3).wait_recv()
     prepare_values(7)
-    blend_last(7, 0)
     for e in (1, 2, 3):
         share(0, e, 6, 6, 1)
+    blend_last(7, 0)
     blend_last(7, 1)
 
-    for copy in x_copies:
-        copy.wait_recv()
+    far_copy.wait_recv()
     length = jnp.zeros((8, 128), jnp.int32)
     for p in range(16):
         length = length + pick(group_of[p] == req, lens[p])
@@ -484,8 +486,8 @@
             dma((SLOTS, 4)),
             dma((16,)),
             dma((16,)),
-            dma((5,)),
-            dma((5,)),
+            dma((4,)),
+            dma((4,)),
         ],
         compiler_params=pltpu.CompilerParams(collective_id=0, has_side_effects=True, vmem_limit_bytes=32 * 2**20),
     )(

time: 104 us -> 104 us (level)
  no operation moved by 1% of the time
where the time goes in v4:
time: 104 us
  Pallas kernels  103 us (99%)
  between operations  1.29 us (1%)
    pallas_call x1, Pallas kernels, on_device(): pl.pallas_call(kernel, out_shape=(jax.ShapeDtypeStruct((rows, wide), bf16...  102 us

profile of v4, /device:TPU:1, one launch (start us, length us, event | category | flops | bytes accessed | tf_op | source)
XLA Modules:
  0.0 104.1 jit_solution(9155425868019044311)
XLA Ops:
  1.3 101.8 %shard_map.86 = (bf16[512,512]{1,0:T(8,128)(2,1)S(1)}, bf16[128,2048]{1,0:T(8,128)(2,1)S(1)}) custom-call(bf16[512,512]{1,0:T(8,128)(2,1)} %bitcast.6, bf16[512,256]{1,0:T(8,128)(2,1)} %bitcast.7, bf16[512,256]{1,0:T(8,128)(2,1)} %bitcast.8, s32[1,2,8]{2,1,0:T(2,128)} %bitcast.9, s32[1]{0:T(128)S(6)} %copy.9.length_ref, s32[16]{0:T(128)} %group_of.1, ...), custom_call_target="tpu_custom_call" | custom-call | tf_op jit(solution)/shard_map/pallas_call | solution.py:457
  103.1 1.0 shard_map.87

commit v5 on v4

--- a/solution.py
+++ b/solution.py
@@ -437,13 +437,20 @@
         copy.wait_send()
 
 
+PIECES = 4
+
+
 def put_out(out_ref, cache_ref, out_to, cache_to, sem):
-    first = pltpu.make_async_copy(out_ref, out_to, sem.at[0])
-    second = pltpu.make_async_copy(cache_ref, cache_to, sem.at[1])
-    first.start()
-    second.start()
-    first.wait()
-    second.wait()
+    copies = []
+    for which, (source, target) in enumerate(((out_ref, out_to), (cache_ref, cache_to))):
+        size = source.shape[0] // PIECES
+        for piece in range(PIECES):
+            rows = pl.ds(piece * size, size)
+            copies.append(pltpu.make_async_copy(source.at[rows], target.at[rows], sem.at[which, piece]))
+    for copy in copies:
+        copy.start()
+    for copy in copies:
+        copy.wait()
 
 
 def on_device(queries, keys, values, block_map, lengths, group_of_prompt, decode_rank):
@@ -504,7 +511,7 @@
         in_specs=[pl.BlockSpec(memory_space=pltpu.VMEM)] * 2,
         compiler_params=pltpu.CompilerParams(vmem_limit_bytes=8 * 2**20),
         out_specs=(pl.BlockSpec(memory_space=pl.ANY),) * 2,
-        scratch_shapes=[dma((2,))],
+        scratch_shapes=[dma((2, PIECES))],
     )(out, cache)
     return out[None, None], cache[None]
 

time: 104 us -> 104 us (level)
  no operation moved by 1% of the time
where the time goes in v5:
time: 104 us
  Pallas kernels  103 us (99%)
  between operations  1.29 us (1%)
    pallas_call x1, Pallas kernels, on_device(): pl.pallas_call(kernel, out_shape=(jax.ShapeDtypeStruct((rows, wide), bf16...  102 us

profile of v5, /device:TPU:1, one launch (start us, length us, event | category | flops | bytes accessed | tf_op | source)
XLA Modules:
  0.0 104.1 jit_solution(15294215920747988835)
XLA Ops:
  1.3 101.8 %shard_map.86 = (bf16[512,512]{1,0:T(8,128)(2,1)S(1)}, bf16[128,2048]{1,0:T(8,128)(2,1)S(1)}) custom-call(bf16[512,512]{1,0:T(8,128)(2,1)} %bitcast.6, bf16[512,256]{1,0:T(8,128)(2,1)} %bitcast.7, bf16[512,256]{1,0:T(8,128)(2,1)} %bitcast.8, s32[1,2,8]{2,1,0:T(2,128)} %bitcast.9, s32[1]{0:T(128)S(6)} %copy.9.length_ref, s32[16]{0:T(128)} %group_of.1, ...), custom_call_target="tpu_custom_call" | custom-call | tf_op jit(solution)/shard_map/pallas_call | solution.py:464
  103.1 1.0 shard_map.87

commit v6 on v3

--- a/solution.py
+++ b/solution.py
@@ -18,6 +18,7 @@
 CAP = 50.0
 QUERY_SCALE = 1.0 / 12.0
 ROPE_BASE = 10000.0
+DEPTH = 3
 ORDER = (0, 1, 7, 2, 6, 3, 5, 4)
 MESH = pl.DeviceIdType.MESH
 
@@ -99,17 +100,12 @@
             device_id_type=MESH,
         )
 
-    def travels(side, turn, chunk):
-        if turn < 3:
-            return True
-        return turn == 3 and (chunk // 2 == side)
-
+    line = [[(step // 4, (step % 4 + 2 * side) % 4) for step in range(14)] for side in range(2)]
+    copies = [[hop(side, *line[side][step]) for step in range(14)] for side in range(2)]
+    for step in range(DEPTH):
+        for side in range(2):
+            copies[side][step].start()
     sent = []
-    for place_in_line in range(4):
-        for side in range(2):
-            copy = hop(side, 0, (place_in_line + 2 * side) % 4)
-            copy.start()
-            sent.append(copy)
 
     lens[req] = jnp.full((8, 128), length_ref[0], jnp.int32)
 
@@ -333,36 +329,56 @@
         prepare(order)
         attend(order, 0)
 
+    def lens_along_y():
+        mate_copy.wait_recv()
+        y_copy.start()
+        sent.append(y_copy)
+
+    def lens_along_x():
+        y_copy.wait_recv()
+        for copy in x_copies:
+            copy.start()
+            sent.append(copy)
+
+    y_copy = len_copy(1, (req // 2) * 2, 2, y_mate)
+    x_copies = [len_copy(2 + i, (req // 4) * 4, 4, x_mates[i]) for i in range(3)]
+
     work = {
-        1: [own_keys_and_first, lambda: attend_own(1), lambda: None, lambda: None],
-        2: [lambda: first_of(1), lambda: attend(1, 1), lambda: first_of(2), lambda: attend(2, 1)],
-        3: [lambda: first_of(3), lambda: attend(3, 1), lambda: first_of(4), lambda: attend(4, 1)],
+        0: [own_keys_and_first],
+        1: [lambda: attend_own(1)],
+        2: [lens_along_y],
+        4: [lens_along_x],
+        5: [lambda: first_of(1)],
+        6: [lambda: attend(1, 1)],
+        7: [lambda: first_of(2)],
+        8: [lambda: attend(2, 1)],
+        9: [lambda: first_of(3), lambda: attend(3, 1)],
+        10: [lambda: first_of(4), lambda: attend(4, 1)],
     }
-    for turn in range(1, 4):
-        for place_in_line in range(4):
+    got = [0]
+
+    def receive(upto):
+        while got[0] <= upto:
             for side in range(2):
-                chunk = (place_in_line + 2 * side) % 4
-                hop(side, turn - 1, chunk).wait_recv()
-                if travels(side, turn, chunk):
-                    copy = hop(side, turn, chunk)
-                    copy.start()
-                    sent.append(copy)
-            if place_in_line == 0 and turn == 2:
-                mate_copy.wait_recv()
-                y_copy = len_copy(1, (req // 2) * 2, 2, y_mate)
-                y_copy.start()
-                sent.append(y_copy)
-            if place_in_line == 0 and turn == 3:
-                y_copy.wait_recv()
-                x_copies = [len_copy(2 + i, (req // 4) * 4, 4, x_mates[i]) for i in range(3)]
-                for copy in x_copies:
-                    copy.start()
-                    sent.append(copy)
-            work[turn][place_in_line]()
+                copies[side][got[0]].wait_recv()
+            got[0] += 1
+
+    for step in range(12):
+        for side in range(2):
+            copies[side][step].wait_send()
+        following = step + DEPTH
+        if following < 14:
+            receive(following - 4)
+            for side in range(2):
+                copies[side][following].start()
+        for unit in work.get(step, []):
+            receive(4 * ((step - 1) // 4) - 1)
+            unit()
     share(0, 1, 0, 0, 5)
     for e in (2, 3):
         share(1, e, 2 - 2 * parity, 1, 2)
         share(0, e, 0, 0, 1)
+    receive(11)
     prepare(5)
     attend(5, 0)
     attend(5, 1)
@@ -374,13 +390,11 @@
         share(0, e, 7, 7, 1)
     for e in (2, 3):
         share(1, e, 4 - 2 * parity, 3, 2)
-    hop(0, 3, 0).wait_recv()
-    hop(1, 3, 2).wait_recv()
+    receive(12)
     prepare_keys(7)
     weigh_last(7, 0)
     weigh_last(7, 1)
-    hop(0, 3, 1).wait_recv()
-    hop(1, 3, 3).wait_recv()
+    receive(13)
     prepare_values(7)
     blend_last(7, 0)
     for e in (1, 2, 3):
@@ -431,6 +445,9 @@
             start = pl.multiple_of(kind * HEAD_DIVISIONS * width + from_head * width, width)
             cache_ref[:, pl.ds(start, width)] = moved[:, kind * width : (kind + 1) * width]
 
+    for step in (12, 13):
+        for side in range(2):
+            copies[side][step].wait_send()
     for copy in sent:
         copy.wait_send()
 

time: 104 us -> 104 us (level)
  no operation moved by 1% of the time
where the time goes in v6:
time: 104 us
  Pallas kernels  103 us (99%)
  between operations  1.29 us (1%)
    pallas_call x1, Pallas kernels, on_device(): pl.pallas_call(kernel, out_shape=(jax.ShapeDtypeStruct((rows, wide), bf16...  102 us

profile of v6, /device:TPU:1, one launch (start us, length us, event | category | flops | bytes accessed | tf_op | source)
XLA Modules:
  0.0 104.2 jit_solution(9014579731555060295)
XLA Ops:
  1.3 101.9 %shard_map.86 = (bf16[512,512]{1,0:T(8,128)(2,1)S(1)}, bf16[128,2048]{1,0:T(8,128)(2,1)S(1)}) custom-call(bf16[512,512]{1,0:T(8,128)(2,1)} %bitcast.6, bf16[512,256]{1,0:T(8,128)(2,1)} %bitcast.7, bf16[512,256]{1,0:T(8,128)(2,1)} %bitcast.8, s32[1,2,8]{2,1,0:T(2,128)} %bitcast.9, s32[1]{0:T(128)S(6)} %copy.9.length_ref, s32[16]{0:T(128)} %group_of.1, ...), custom_call_target="tpu_custom_call" | custom-call | tf_op jit(solution)/shard_map/pallas_call | solution.py:472
  103.2 1.0 shard_map.87
